TPU v7x, 32 devices: a whole 2x2x4 slice. The times are simulated.
32 devices in a mesh: dp: 32 (over z, y, x, core).
Axes of the slice: x: 2, y: 2, z: 4, core: 2. Of those that a mesh axis runs over, the one named last changes fastest.
Arguments:
- tokens: bfloat16 [32768, 768], P('dp'), may hold values from -6 to 6
- cotangent: bfloat16 [32768, 768], P('dp'), may hold values from -6 to 6
- cluster_order: int32 [32768], P('dp'), may hold values from 0 to 1023, as said below
- live_clusters: int32 [32], P('dp'), may hold values from 4 to 8, as said below
- step_count: int32 [1], replicated, may hold values from 1 to 20
- learn_rates: float32 [6], replicated, may hold values from 0.4 to 1
- w_qkv: float32 [768, 2304], P('dp'), may hold values from -0.21875 to 0.21875
- w_out: float32 [768, 768], P('dp'), may hold values from -2.5 to 2.5
- w_up: float32 [768, 3072], P('dp'), may hold values from -0.21875 to 0.21875
- w_down: float32 [3072, 768], P('dp'), may hold values from -0.109375 to 0.109375
- biases: float32 [7680], P('dp'), may hold values from -1.2 to 1.2
- norm_gains: float32 [1536], P('dp'), may hold values from 0.5 to 1.5
- m_qkv: float32 [768, 2304], P('dp'), may hold values from -0.00024414062 to 0.00024414062
- m_out: float32 [768, 768], P('dp'), may hold values from -4.5776367e-05 to 4.5776367e-05
- m_up: float32 [768, 3072], P('dp'), may hold values from -0.00012207031 to 0.00012207031
- m_down: float32 [3072, 768], P('dp'), may hold values from -0.00030517578 to 0.00030517578
- m_biases: float32 [7680], P('dp'), may hold values from -0.00030517578 to 0.00030517578
- m_gains: float32 [1536], P('dp'), may hold values from -0.00061035156 to 0.00061035156
- v_qkv: float32 [768, 2304], P('dp'), may hold values from 1.6349286e-10 to 6.5612266e-10
- v_out: float32 [768, 768], P('dp'), may hold values from 4.9865325e-12 to 1.994613e-11
- v_up: float32 [768, 3072], P('dp'), may hold values from 4.0873215e-11 to 1.6349286e-10
- v_down: float32 [3072, 768], P('dp'), may hold values from 2.544149e-10 to 1.0176596e-09
- v_biases: float32 [7680], P('dp'), may hold values from 2.544149e-10 to 1.0176596e-09
- v_gains: float32 [1536], P('dp'), may hold values from 1.0176596e-09 to 3.989226e-09
Outputs:
- output: bfloat16 [32768, 768], P('dp')
- input_grad: bfloat16 [32768, 768], P('dp')
- grad_norm: float32 [1], replicated
- new_m_qkv: float32 [768, 2304], P('dp')
- new_m_out: float32 [768, 768], P('dp')
- new_m_up: float32 [768, 3072], P('dp')
- new_m_down: float32 [3072, 768], P('dp')
- new_m_biases: float32 [7680], P('dp')
- new_m_gains: float32 [1536], P('dp')
- new_v_qkv: float32 [768, 2304], P('dp')
- new_v_out: float32 [768, 768], P('dp')
- new_v_up: float32 [768, 3072], P('dp')
- new_v_down: float32 [3072, 768], P('dp')
- new_v_biases: float32 [7680], P('dp')
- new_v_gains: float32 [1536], P('dp')
- new_w_qkv: float32 [768, 2304], P('dp')
- new_w_out: float32 [768, 768], P('dp')
- new_w_up: float32 [768, 3072], P('dp')
- new_w_down: float32 [3072, 768], P('dp')
- new_biases: float32 [7680], P('dp')
- new_gains: float32 [1536], P('dp')
Inputs may be any that keep to these rules, and one draw needn't show every extreme that they name: `cluster_order`: on each device, a permutation of 0 to 1023. The device's items lie end to end from row 0, each 512 rows (short) or 1024 rows (long); the permutation keeps every item's rows inside the item and keeps dead rows among dead rows. The clusters of a device that hold item rows, a multiple of 4; its first live_clusters * 128 reordered rows are live. Some device holds 8.
All inputs are finite; a program needn't handle non-finite values.
Results may differ from a plain program's by a relative error of at most 0.015.
The roundings to bfloat16 on the way count: a program that leaves them out, or rounds other values in their place, can miss the bound.
Values may be sent and summed in bfloat16 or wider, within the bound.
No kernel may reach another device: no remote copies, remote signals or barrier semaphores. Data moves between devices by JAX's collectives and lax.ppermute only.
A program may use at most 256 MiB of HBM per device.

v0:
```python
import jax
import jax.numpy as jnp
from jax import lax
from jax.sharding import PartitionSpec as P

D = 768
HEADS = 12
HEAD_DIM = 64
FF = 3072
CLUSTER = 128
SHORT_CL = 4


EPSILON = 1e-06
CLIP_BOUND = 1.0
BETA_ONE = 0.9
BETA_TWO = 0.999
ADAM_EPS = 1e-08
DECAY = 0.01


def shortened(value):
    return jax.tree.map(lambda a: a.astype(jnp.bfloat16) if a.dtype == jnp.float32 else a, value)


def split_vectors(bias_all, gain_all):
    model_width = gain_all.shape[0] // 2
    hidden_width = bias_all.shape[0] - 6 * model_width
    bounds = (
        0,
        model_width,
        2 * model_width,
        3 * model_width,
        3 * model_width + hidden_width,
        4 * model_width + hidden_width,
        5 * model_width + hidden_width,
        6 * model_width + hidden_width,
    )
    pieces = tuple((bias_all[bounds[number] : bounds[number + 1]] for number in range(7)))
    return pieces + (gain_all[:model_width], gain_all[model_width:])


def layer_norm(values, gain_vec, shift_vec):
    centred = values - jnp.mean(values, axis=-1, keepdims=True)
    spread = jnp.mean(centred * centred, axis=-1, keepdims=True)
    return centred * lax.rsqrt(spread + EPSILON) * gain_vec + shift_vec


def exact_gelu(values):
    return jax.nn.gelu(values, approximate=False)


def split_heads(qkv_low):
    clusters_here = qkv_low.shape[0] // CLUSTER
    shaped = qkv_low.reshape(clusters_here, CLUSTER, 3, HEADS, HEAD_DIM)
    return (shaped[:, :, 0], shaped[:, :, 1], shaped[:, :, 2])


def cluster_scores(query_low, key_low):
    raw = jnp.einsum("cqhe,ckhe->chqk", query_low, key_low, preferred_element_type=jnp.float32)
    return raw * HEAD_DIM ** (-0.5)


def forward_block(weights, x_block):
    w_qkv, w_out, w_up, w_down, bias_all, gain_all = weights
    b_query, b_value, b_out, b_up, b_down, shift_one, shift_two, gain_one, gain_two = split_vectors(
        bias_all.astype(jnp.float32), gain_all.astype(jnp.float32)
    )
    row_count, model_width = x_block.shape
    qkv_bias = jnp.concatenate([b_query, jnp.zeros_like(b_query), b_value])
    qkv_low = (jnp.dot(x_block, w_qkv, preferred_element_type=jnp.float32) + qkv_bias).astype(
        jnp.bfloat16
    )
    query_low, key_low, value_low = split_heads(qkv_low)
    scaled = cluster_scores(query_low, key_low)
    row_top = jnp.max(scaled, axis=-1, keepdims=True)
    log_total = row_top + jnp.log(jnp.sum(jnp.exp(scaled - row_top), axis=-1, keepdims=True))
    probs_low = jnp.exp(scaled - log_total).astype(jnp.bfloat16)
    context = jnp.einsum(
        "chqk,ckhe->cqhe", probs_low, value_low, preferred_element_type=jnp.float32
    )
    context_low = context.reshape(row_count, model_width).astype(jnp.bfloat16)
    attn_out = jnp.dot(context_low, w_out, preferred_element_type=jnp.float32) + b_out
    first_sum = x_block.astype(jnp.float32) + attn_out
    normed_one = layer_norm(first_sum, gain_one, shift_one)
    up_value = (
        jnp.dot(normed_one.astype(jnp.bfloat16), w_up, preferred_element_type=jnp.float32) + b_up
    )
    hidden_low = exact_gelu(up_value).astype(jnp.bfloat16)
    ffn_out = jnp.dot(hidden_low, w_down, preferred_element_type=jnp.float32) + b_down
    second_sum = normed_one + ffn_out
    result = layer_norm(second_sum, gain_two, shift_two)
    return (result, (qkv_low, log_total, context_low, first_sum, normed_one, up_value, second_sum))


def backward_tail(weights, tail_values, cot_block):
    w_qkv, w_out, w_up, w_down, bias_all, gain_all = weights
    b_query, b_value, b_out, b_up, b_down, shift_one, shift_two, gain_one, gain_two = split_vectors(
        bias_all.astype(jnp.float32), gain_all.astype(jnp.float32)
    )
    context_low, first_sum, normed_one, up_value, second_sum = tail_values
    model_width = first_sum.shape[1]
    unused_two, norm_two_back = jax.vjp(layer_norm, second_sum, gain_two, shift_two)
    d_second, d_gain_two, d_shift_two = norm_two_back(cot_block)
    d_ffn = d_second.astype(jnp.bfloat16)
    hidden_low = exact_gelu(up_value).astype(jnp.bfloat16)
    grad_down = jnp.einsum("rf,rd->fd", hidden_low, d_ffn, preferred_element_type=jnp.float32)
    d_hidden = jnp.einsum("rd,fd->rf", d_ffn, w_down, preferred_element_type=jnp.float32)
    unused_gelu, gelu_back = jax.vjp(exact_gelu, up_value)
    d_up = gelu_back(d_hidden)[0].astype(jnp.bfloat16)
    normed_low = normed_one.astype(jnp.bfloat16)
    grad_up = jnp.einsum("rd,rf->df", normed_low, d_up, preferred_element_type=jnp.float32)
    d_normed = d_second + jnp.einsum("rf,df->rd", d_up, w_up, preferred_element_type=jnp.float32)
    unused_one, norm_one_back = jax.vjp(layer_norm, first_sum, gain_one, shift_one)
    d_first, d_gain_one, d_shift_one = norm_one_back(d_normed)
    d_attn = d_first.astype(jnp.bfloat16)
    grad_out = jnp.einsum("rd,re->de", context_low, d_attn, preferred_element_type=jnp.float32)
    d_context = jnp.einsum("re,de->rd", d_attn, w_out, preferred_element_type=jnp.float32).astype(
        jnp.bfloat16
    )
    bias_tail = jnp.concatenate(
        [
            jnp.zeros((2 * model_width,), jnp.float32),
            jnp.sum(d_attn.astype(jnp.float32), axis=0),
            jnp.sum(d_up.astype(jnp.float32), axis=0),
            jnp.sum(d_ffn.astype(jnp.float32), axis=0),
            d_shift_one,
            d_shift_two,
        ]
    )
    grad_gain = jnp.concatenate([d_gain_one, d_gain_two])
    return (d_first, d_context, (grad_out, grad_up, grad_down, bias_tail, grad_gain))


def backward_head(w_qkv, qkv_low, log_total, x_block, d_first, d_context, bias_length):
    row_count, model_width = x_block.shape
    query_low, key_low, value_low = split_heads(qkv_low)
    d_context = d_context.reshape(query_low.shape)
    probs_full = jnp.exp(cluster_scores(query_low, key_low) - log_total)
    probs_low = probs_full.astype(jnp.bfloat16)
    d_probs = jnp.einsum(
        "cqhe,ckhe->chqk", d_context, value_low, preferred_element_type=jnp.float32
    )
    d_value = jnp.einsum(
        "chqk,cqhe->ckhe", probs_low, d_context, preferred_element_type=jnp.float32
    )
    d_scores = probs_full * (d_probs - jnp.sum(probs_full * d_probs, axis=-1, keepdims=True))
    d_raw = (d_scores * HEAD_DIM ** (-0.5)).astype(jnp.bfloat16)
    d_query = jnp.einsum("chqk,ckhe->cqhe", d_raw, key_low, preferred_element_type=jnp.float32)
    d_key = jnp.einsum("chqk,cqhe->ckhe", d_raw, query_low, preferred_element_type=jnp.float32)
    d_qkv = (
        jnp.stack([d_query, d_key, d_value], axis=2)
        .reshape(row_count, 3 * model_width)
        .astype(jnp.bfloat16)
    )
    grad_qkv = jnp.einsum("rd,re->de", x_block, d_qkv, preferred_element_type=jnp.float32)
    d_input = d_first + jnp.einsum("re,de->rd", d_qkv, w_qkv, preferred_element_type=jnp.float32)
    column_sums = jnp.sum(d_qkv.astype(jnp.float32), axis=0)
    bias_head = jnp.concatenate(
        [
            column_sums[:model_width],
            column_sums[2 * model_width :],
            jnp.zeros((bias_length - 2 * model_width,), jnp.float32),
        ]
    )
    return (d_input, (grad_qkv, bias_head))


def log_rows(log_total):
    return jnp.transpose(log_total[..., 0], (0, 2, 1)).reshape(-1, HEADS)


def log_clusters(per_row):
    return jnp.transpose(per_row.reshape(-1, CLUSTER, HEADS), (0, 2, 1))[..., None]


def adam_update(masters, firsts, seconds, grads, grad_norm, step_count, learn_rates):
    factor = CLIP_BOUND / jnp.maximum(grad_norm, CLIP_BOUND)
    moment = step_count[0].astype(jnp.float32)
    first_fix = 1.0 - BETA_ONE**moment
    second_fix = 1.0 - BETA_TWO**moment
    base_rates = (D ** (-0.5), (D // CLUSTER) ** (-0.5), D ** (-0.5), FF ** (-0.5), 0.5, 0.5)
    new_firsts = []
    new_seconds = []
    new_masters = []
    for number in range(6):
        clipped = factor * grads[number]
        first_new = BETA_ONE * firsts[number] + (1.0 - BETA_ONE) * clipped
        second_new = BETA_TWO * seconds[number] + (1.0 - BETA_TWO) * clipped * clipped
        step_rate = learn_rates[number] * base_rates[number]
        update = (
            first_new / first_fix / (jnp.sqrt(second_new / second_fix) + ADAM_EPS)
            + DECAY * masters[number]
        )
        new_firsts.append(first_new)
        new_seconds.append(second_new)
        new_masters.append(masters[number] - step_rate * update)
    return (new_firsts, new_seconds, new_masters)


def body(
    tokens,
    cotangent,
    cluster_order,
    live_clusters,
    step_count,
    learn_rates,
    w_qkv,
    w_out,
    w_up,
    w_down,
    biases,
    norm_gains,
    m_qkv,
    m_out,
    m_up,
    m_down,
    m_biases,
    m_gains,
    v_qkv,
    v_out,
    v_up,
    v_down,
    v_biases,
    v_gains,
):
    masters = (w_qkv, w_out, w_up, w_down, biases, norm_gains)
    lowered = tuple((master.astype(jnp.bfloat16) for master in masters))
    row_count = tokens.shape[0]
    model_width = tokens.shape[1]
    inverse = (
        jnp.zeros((row_count,), jnp.int32)
        .at[cluster_order]
        .set(jnp.arange(row_count, dtype=jnp.int32))
    )
    ordered = jnp.take(tokens, cluster_order, axis=0)
    ordered_cot = jnp.take(cotangent, cluster_order, axis=0).astype(jnp.float32)
    block_rows = SHORT_CL * CLUSTER
    block_count = live_clusters[0] // SHORT_CL
    gathered = jax.tree.map(
        lambda part, own: part.astype(own.dtype),
        lax.all_gather(shortened(lowered), "dp", axis=0, tiled=True),
        lowered,
    )
    bias_length = gathered[4].shape[0]
    tail_zero = tuple((jnp.zeros(weight_item.shape, jnp.float32) for weight_item in gathered[1:]))
    head_zero = (jnp.zeros(gathered[0].shape, jnp.float32), jnp.zeros((bias_length,), jnp.float32))
    empty_rows = jnp.zeros((row_count, model_width), jnp.float32)
    qkv_init = jnp.zeros((row_count, 3 * model_width), jnp.bfloat16)
    log_init = jnp.zeros((row_count, HEADS), jnp.float32)
    context_init = jnp.zeros((row_count, model_width), jnp.bfloat16)

    def read_rows(source, block_index):
        return lax.dynamic_slice_in_dim(source, block_index * block_rows, block_rows, 0)

    def write_rows(target, value, block_index):
        return lax.dynamic_update_slice_in_dim(target, value, block_index * block_rows, 0)

    hidden_width = gathered[2].shape[1]
    stores_init = (
        jnp.zeros((row_count, model_width), jnp.bfloat16),
        jnp.zeros((row_count, model_width), jnp.float32),
        jnp.zeros((row_count, model_width), jnp.float32),
        jnp.zeros((row_count, hidden_width), jnp.float32),
        jnp.zeros((row_count, model_width), jnp.float32),
    )

    def forward_step(block_index, loop_state):
        results, qkv_store, log_store, stores = loop_state
        result, kept_values = forward_block(gathered, read_rows(ordered, block_index))
        stores = tuple(
            (
                write_rows(target, value, block_index)
                for target, value in zip(stores, kept_values[2:])
            )
        )
        return (
            write_rows(results, result, block_index),
            write_rows(qkv_store, kept_values[0], block_index),
            write_rows(log_store, log_rows(kept_values[1]), block_index),
            stores,
        )

    results, qkv_store, log_store, stores = lax.fori_loop(
        0, block_count, forward_step, (empty_rows, qkv_init, log_init, stores_init)
    )
    regathered = jax.tree.map(
        lambda part, own: part.astype(own.dtype),
        lax.all_gather(shortened(lowered), "dp", axis=0, tiled=True),
        lowered,
    )

    def tail_step(block_index, loop_state):
        first_store, dctx_store, totals = loop_state
        tail_values = tuple((read_rows(source, block_index) for source in stores))
        d_first, d_context, block_grads = backward_tail(
            regathered, tail_values, read_rows(ordered_cot, block_index)
        )
        totals = tuple((running + addend for running, addend in zip(totals, block_grads)))
        return (
            write_rows(first_store, d_first, block_index),
            write_rows(dctx_store, d_context, block_index),
            totals,
        )

    first_store, dctx_store, tail_totals = lax.fori_loop(
        0, block_count, tail_step, (empty_rows, context_init, tail_zero)
    )
    head_weight = regathered[0]

    def head_step(block_index, loop_state):
        input_grads, totals = loop_state
        d_input, block_grads = backward_head(
            head_weight,
            read_rows(qkv_store, block_index),
            log_clusters(read_rows(log_store, block_index)),
            read_rows(ordered, block_index),
            read_rows(first_store, block_index),
            read_rows(dctx_store, block_index),
            bias_length,
        )
        totals = tuple((running + addend for running, addend in zip(totals, block_grads)))
        return (write_rows(input_grads, d_input, block_index), totals)

    input_grads, head_totals = lax.fori_loop(0, block_count, head_step, (empty_rows, head_zero))
    totals = (
        head_totals[0],
        tail_totals[0],
        tail_totals[1],
        tail_totals[2],
        tail_totals[3] + head_totals[1],
        tail_totals[4],
    )
    reduced = (
        lax.psum_scatter(totals[0], "dp", scatter_dimension=0, tiled=True),
        lax.psum_scatter(totals[1], "dp", scatter_dimension=0, tiled=True),
        lax.psum_scatter(totals[2], "dp", scatter_dimension=0, tiled=True),
        lax.psum_scatter(totals[3], "dp", scatter_dimension=0, tiled=True),
        lax.psum_scatter(totals[4], "dp", scatter_dimension=0, tiled=True),
        lax.psum_scatter(totals[5], "dp", scatter_dimension=0, tiled=True),
    )
    output = jnp.take(results, inverse, axis=0).astype(jnp.bfloat16)
    input_grad = jnp.take(input_grads, inverse, axis=0).astype(jnp.bfloat16)
    local_squares = jnp.sum(jnp.stack([jnp.sum(grad_item * grad_item) for grad_item in reduced]))
    total_squares = lax.psum(local_squares, "dp")
    grad_norm = jnp.sqrt(total_squares)
    firsts, seconds, updated = adam_update(
        masters,
        (m_qkv, m_out, m_up, m_down, m_biases, m_gains),
        (v_qkv, v_out, v_up, v_down, v_biases, v_gains),
        reduced,
        grad_norm,
        step_count,
        learn_rates,
    )
    return (
        output,
        input_grad,
        grad_norm.reshape(1),
        firsts[0],
        firsts[1],
        firsts[2],
        firsts[3],
        firsts[4],
        firsts[5],
        seconds[0],
        seconds[1],
        seconds[2],
        seconds[3],
        seconds[4],
        seconds[5],
        updated[0],
        updated[1],
        updated[2],
        updated[3],
        updated[4],
        updated[5],
    )


def solution(mesh):
    return jax.shard_map(
        body,
        mesh=mesh,
        in_specs=(
            P("dp", None),
            P("dp", None),
            P("dp"),
            P("dp"),
            P(),
            P(),
            P("dp", None),
            P("dp", None),
            P("dp", None),
            P("dp", None),
            P("dp"),
            P("dp"),
            P("dp", None),
            P("dp", None),
            P("dp", None),
            P("dp", None),
            P("dp"),
            P("dp"),
            P("dp", None),
            P("dp", None),
            P("dp", None),
            P("dp", None),
            P("dp"),
            P("dp"),
        ),
        out_specs=(
            P("dp", None),
            P("dp", None),
            P(),
            P("dp", None),
            P("dp", None),
            P("dp", None),
            P("dp", None),
            P("dp"),
            P("dp"),
            P("dp", None),
            P("dp", None),
            P("dp", None),
            P("dp", None),
            P("dp"),
            P("dp"),
            P("dp", None),
            P("dp", None),
            P("dp", None),
            P("dp", None),
            P("dp"),
            P("dp"),
        ),
        check_vma=False,
    )
```

profile of v0, /device:TPU:0, one launch (start us, length us, event | category | flops | bytes accessed | tf_op | source)
XLA Modules:
  0.0 1135.4 jit_solution(15992560120229841577)
XLA Ops:
  16.6 5.2 gather_fusion
  21.8 7.3 gather_fusion.2
  29.6 42.3 %all-reduce.5 = (bf16[7680]{0:T(1024)(128)(2,1)S(1)}, bf16[1536]{0:T(1024)(128)(2,1)S(1)}) all-reduce(bf16[7680]{0:T(1024)(128)(2,1)S(1)} %dynamic-update-slice, bf16[1536]{0:T(1024)(128)(2,1)S(1)} %dynamic-update-slice.1), channel_id=1, replica_groups=mesh['dp'=32] {'dp'}, use_global_device_ids=true, to_apply=%add | all-reduce | flops 9216 | bytes 36864
  75.8 55.0 %all-gather.5.cloned.1.call-done = bf16[768,2304]{1,0:T(8,128)(2,1)} async-done(((bf16[24,2304]{1,0:T(8,128)(2,1)}), bf16[768,2304]{1,0:T(8,128)(2,1)}) %all-gather.5.cloned.1.call-update) | async-done | bytes 3538960 | tf_op jit(solution)/shard_map/all_gather | solution.py:242
  130.8 65.9 %all-gather.11.cloned.1.call-done = bf16[3072,768]{1,0:T(8,128)(2,1)} async-done(((bf16[96,768]{1,0:T(8,128)(2,1)}), bf16[3072,768]{1,0:T(8,128)(2,1)}) %all-gather.11.cloned.1.call-update) | async-done | bytes 4718608 | tf_op jit(solution)/shard_map/all_gather | solution.py:242
  196.7 65.3 %all-gather.9.cloned.1.call-done = bf16[768,3072]{1,0:T(8,128)(2,1)} async-done(((bf16[24,3072]{1,0:T(8,128)(2,1)}), bf16[768,3072]{1,0:T(8,128)(2,1)}) %all-gather.9.cloned.1.call-update) | async-done | bytes 4718608 | tf_op jit(solution)/shard_map/all_gather | solution.py:242
  262.0 6.1 broadcast_in_dim.67
  275.6 125.3 %while.60 = (s32[]{:T(128)}, bf16[1024,768]{1,0:T(8,128)(2,1)S(1)}, bf16[1024,2304]{1,0:T(8,128)(2,1)}, f32[1024,12]{0,1:T(8,128)S(1)}, bf16[1024,768]{0,1:T(8,1...) while((s32[]{:T(128)}, bf16[1024,768]{1,0:T(8,128)(2,1)S(1)}, ...), condition=%wide.region_7.9_spmd, body=%wide.region_0.8_spmd.sunk | while | flops 7575305728 | bytes 229473856 | solution.py:284
  293.7 6.4 constant_dynamic-update-slice_fusion.18
  300.1 4.3 copy.179
  304.4 5.3 reshape.273
  321.4 16.0 %fusion.225 = (f32[512]{0:T(512)S(1)}, f32[512,768]{1,0:T(8,128)S(1)}) fusion(f32[768]{0:T(1024)S(1)} %get-tuple-element.908, bf16[3072,768]{1,0:T(8,128)(2,1)S(1)} %bitcast.190, f32[512,3072]{1,0:T(8,128)S(1)} %get-tuple-element.909, f32[3072]{0:T(1024)S(1)} %slice.170, f32[768]{0:T(1024)S(1)} %get-tuple-element.903, ...), kind=kOutput, calls=%fused_computation.259.clone.1 | convolution fusion | flops 2522480128 | bytes 14183424 | tf_op jit(solution)/shard_map/while/body/dot_general | solution.py:90
  341.3 6.4 constant_dynamic-update-slice_fusion.18
  347.7 4.3 copy.179
  352.1 5.3 reshape.273
  369.1 16.0 %fusion.225 = (f32[512]{0:T(512)S(1)}, f32[512,768]{1,0:T(8,128)S(1)}) fusion(f32[768]{0:T(1024)S(1)} %get-tuple-element.908, bf16[3072,768]{1,0:T(8,128)(2,1)S(1)} %bitcast.190, f32[512,3072]{1,0:T(8,128)S(1)} %get-tuple-element.909, f32[3072]{0:T(1024)S(1)} %slice.170, f32[768]{0:T(1024)S(1)} %get-tuple-element.903, ...), kind=kOutput, calls=%fused_computation.259.clone.1 | convolution fusion | flops 2522480128 | bytes 14183424 | tf_op jit(solution)/shard_map/while/body/dot_general | solution.py:90
  400.9 4.7 broadcast_in_dim.82
  405.7 4.3 broadcast_in_dim.83
  414.7 131.5 %while.61 = (s32[]{:T(128)}, f32[1024,768]{1,0:T(8,128)}, bf16[1024,768]{1,0:T(8,128)(2,1)}, f32[768,768]{1,0:T(8,128)}, f32[768,3072]{1,0:T(8,128)}, /*index=5*...) while((s32[]{:T(128)}, f32[1024,768]{1,0:T(8,128)}, ...), condition=%wide.region_25.28_spmd, body=%wide.region_9.27_spmd.sunk | while | flops 11017333760 | bytes 293263008 | solution.py:306
  425.4 19.0 %convert_reduce_fusion.9 = (f32[3072]{0:T(1024)S(1)}, bf16[512,3072]{1,0:T(8,128)(2,1)S(1)}, f32[512,3072]{1,0:T(8,128)}) fusion(f32[1024,3072]{1,0:T(8,128)S(1)} %copy-done.6, s32[]{:T(128)S(6)} %select_n.82, bf16[512,768]{1,0:T(8,128)(2,1)S(1)} %get-tuple-element.943, bf16[3072,768]{1,0:T(8,128)(2,1)} %get-tuple-element.1102), kind=kOutput, calls=%fused_computation.102.clone.1 | convolution fusion | flops 2532307968 | bytes 21245956 | tf_op jit(solution)/shard_map/while/body/rd,fd->rf/dot_general | solution.py:108
  444.4 5.7 multiply_reduce_fusion.27
  454.5 14.2 %convolution_add_fusion.11 = f32[3072,768]{1,0:T(8,128)} fusion(f32[3072,768]{1,0:T(8,128)} %get-tuple-element.1071, bf16[512,768]{1,0:T(8,128)(2,1)S(1)} %get-tuple-element.943, f32[512,3072]{1,0:T(8,128)} %get-tuple-element.951, f32[1024,3072]{1,0:T(8,128)} %get-tuple-element.1101, s32[]{:T(128)S(6)} %select_n.82), kind=kOutput, calls=%fused_computation.118.clone.1 | convolution fusion | flops 2422996992 | bytes 32243716 | tf_op jit(solution)/shard_map/while/body/rf,rd->fd/dot_general | solution.py:107
  470.7 7.5 convolution_add_fusion.10
  491.0 19.0 %convert_reduce_fusion.9 = (f32[3072]{0:T(1024)S(1)}, bf16[512,3072]{1,0:T(8,128)(2,1)S(1)}, f32[512,3072]{1,0:T(8,128)}) fusion(f32[1024,3072]{1,0:T(8,128)S(1)} %copy-done.6, s32[]{:T(128)S(6)} %select_n.82, bf16[512,768]{1,0:T(8,128)(2,1)S(1)} %get-tuple-element.943, bf16[3072,768]{1,0:T(8,128)(2,1)} %get-tuple-element.1102), kind=kOutput, calls=%fused_computation.102.clone.1 | convolution fusion | flops 2532307968 | bytes 21245956 | tf_op jit(solution)/shard_map/while/body/rd,fd->rf/dot_general | solution.py:108
  510.0 5.7 multiply_reduce_fusion.27
  520.1 14.2 %convolution_add_fusion.11 = f32[3072,768]{1,0:T(8,128)} fusion(f32[3072,768]{1,0:T(8,128)} %get-tuple-element.1071, bf16[512,768]{1,0:T(8,128)(2,1)S(1)} %get-tuple-element.943, f32[512,3072]{1,0:T(8,128)} %get-tuple-element.951, f32[1024,3072]{1,0:T(8,128)} %get-tuple-element.1101, s32[]{:T(128)S(6)} %select_n.82), kind=kOutput, calls=%fused_computation.118.clone.1 | convolution fusion | flops 2422996992 | bytes 32243716 | tf_op jit(solution)/shard_map/while/body/rf,rd->fd/dot_general | solution.py:107
  536.2 7.5 convolution_add_fusion.10
  549.6 121.1 %while.62 = (s32[]{:T(128)}, bf16[1024,768]{1,0:T(8,128)(2,1)S(1)}, f32[768,2304]{1,0:T(8,128)}, f32[7680]{0:T(1024)S(1)}, s32[]{:T(128)}, /*index=5*/f32[1024,7...) while((s32[]{:T(128)}, bf16[1024,768]{1,0:T(8,128)(2,1)S(1)}, ...), condition=%wide.region_29.32_spmd, body=%wide.region_26.31_spmd.sunk | while | flops 4150624768 | bytes 138390960 | solution.py:325
  552.8 4.4 copy.192
  557.2 5.3 reshape.274
  575.7 7.5 fusion.257
  583.2 7.2 fusion.256
  595.8 4.0 copy.195
  599.9 8.2 convolution_add_fusion.12
  613.4 4.3 copy.192
  617.8 5.3 reshape.274
  636.2 7.4 fusion.257
  643.6 7.2 fusion.256
  660.2 8.1 convolution_add_fusion.12
  677.5 4.4 scatter_custom_fusion
  682.0 5.2 gather_fusion.3
  687.2 5.2 gather_fusion.1
  692.4 40.1 %all-reduce.4 = (f32[7680]{0:T(1024)S(1)}, f32[1536]{0:T(1024)S(1)}) all-reduce(f32[7680]{0:T(1024)S(1)} %add.296, f32[1536]{0:T(1024)S(1)} %get-tuple-element.299), channel_id=6, replica_groups=mesh['dp'=32] {'dp'}, use_global_device_ids=true, to_apply=%region_38.41.clone | all-reduce | flops 9216 | bytes 73728
  735.3 54.1 %reduce-scatter.5.cloned.1.call-done = f32[24,2304]{1,0:T(8,128)} async-done(((f32[768,2304]{1,0:T(8,128)}), f32[24,2304]{1,0:T(8,128)}) %reduce-scatter.5.cloned.1.call-update) | async-done | bytes 221200 | tf_op jit(solution)/shard_map/reduce_scatter | solution.py:335
  792.4 138.2 %reduce-scatter.9.cloned.1.call-done = f32[24,3072]{1,0:T(8,128)} async-done(((f32[768,3072]{1,0:T(8,128)}), f32[24,3072]{1,0:T(8,128)}) %reduce-scatter.9.cloned.1.call-update) | async-done | bytes 294928 | tf_op jit(solution)/shard_map/reduce_scatter | solution.py:337
  932.8 138.8 %reduce-scatter.11.cloned.1.call-done = f32[96,768]{1,0:T(8,128)} async-done(((f32[3072,768]{1,0:T(8,128)}), f32[96,768]{1,0:T(8,128)}) %reduce-scatter.11.cloned.1.call-update) | async-done | bytes 294928 | tf_op jit(solution)/shard_map/reduce_scatter | solution.py:338
  1075.4 4.3 select_convert_fusion
  1079.7 39.6 %psum.7 = f32[]{:T(128)} all-reduce(f32[]{:T(128)S(6)} %reduce_sum.313), channel_id=1, replica_groups=mesh['dp'=32] {'dp'}, use_global_device_ids=true, to_apply=%region_42.45 | all-reduce | flops 1 | bytes 8 | tf_op jit(solution)/shard_map/psum | solution.py:345
  (411 shorter events, 166.2 us)
Async XLA Ops:
  7.2 9.4 copy-start
  7.2 68.6 %all-gather.7.cloned.1.call-start = ((), (), s32[]{:S(2)}) async-start(), calls=%async_computation.5 | async-start | bytes 1216512 | tf_op jit(solution)/shard_map/all_gather | solution.py:242
  8.9 121.9 %all-gather.5.cloned.1.call-start = ((), (), s32[]{:S(2)}) async-start(), calls=%async_computation.4 | async-start | bytes 3649536 | tf_op jit(solution)/shard_map/all_gather | solution.py:242
  10.6 186.1 %all-gather.11.cloned.1.call-start = ((), (), s32[]{:S(2)}) async-start(), calls=%async_computation.7 | async-start | bytes 4866048 | tf_op jit(solution)/shard_map/all_gather | solution.py:242
  12.3 249.7 %all-gather.9.cloned.1.call-start = ((), (), s32[]{:S(2)}) async-start(), calls=%async_computation.6 | async-start | bytes 4866048 | tf_op jit(solution)/shard_map/all_gather | solution.py:242
  14.0 719.8 %reduce-scatter.7.cloned.1.call-start = ((), (), s32[]{:S(2)}) async-start(), calls=%async_computation.9 | async-start | bytes 2433024 | tf_op jit(solution)/shard_map/reduce_scatter | solution.py:336
  21.8 7.3 copy-start.46
  21.8 7.3 copy-start.50
  21.8 50.1 %copy-start.25 = (bf16[1024,768]{1,0:T(8,128)(2,1)S(1)}, bf16[1024,768]{1,0:T(8,128)(2,1)}, u32[]{:S(2)}) copy-start(bf16[1024,768]{1,0:T(8,128)(2,1)} %gather_fusion) | copy-start | bytes 4718596
  309.7 7.8 slice-start.5
  321.3 16.0 %copy-start.5 = (f32[1024,3072]{1,0:T(8,128)}, f32[1024,3072]{1,0:T(8,128)S(1)}, u32[]{:S(2)}) copy-start(f32[1024,3072]{1,0:T(8,128)S(1)} %get-tuple-element.1028) | copy-start | bytes 37748740 | tf_op jit(solution)/shard_map/while
  357.3 7.8 slice-start.5
  369.0 16.0 %copy-start.5 = (f32[1024,3072]{1,0:T(8,128)}, f32[1024,3072]{1,0:T(8,128)S(1)}, u32[]{:S(2)}) copy-start(f32[1024,3072]{1,0:T(8,128)S(1)} %get-tuple-element.1028) | copy-start | bytes 37748740 | tf_op jit(solution)/shard_map/while
  422.9 21.5 %slice-start.7 = ((s8[4718592]{0:T(1024)(128)(4,1)}), s8[4194304]{0:T(1024)(128)(4,1)S(1)}, s32[]{:S(2)}) async-start(s8[4718592]{0:T(1024)(128)(4,1)} %bitcast.193), calls=%async_computation.19 | async-start | bytes 8388608 | tf_op jit(solution)/shard_map/while
  425.4 19.0 %slice-start.8 = ((s8[4718592]{0:T(1024)(128)(4,1)}), s8[524288]{0:T(1024)(128)(4,1)S(1)}, s32[]{:S(2)}) async-start(s8[4718592]{0:T(1024)(128)(4,1)} %bitcast.193), calls=%async_computation.20 | async-start | bytes 1048576 | tf_op jit(solution)/shard_map/while
  454.5 14.2 %copy-start.9 = (f32[768,768]{1,0:T(8,128)S(1)}, f32[768,768]{1,0:T(8,128)}, u32[]{:S(2)}) copy-start(f32[768,768]{1,0:T(8,128)} %get-tuple-element.1069) | copy-start | bytes 7077892 | tf_op jit(solution)/shard_map/while
  454.5 14.2 %copy-start.21 = (bf16[1024,768]{0,1:T(8,128)(2,1)S(1)}, bf16[1024,768]{0,1:T(8,128)(2,1)}, u32[]{:S(2)}) copy-start(bf16[1024,768]{0,1:T(8,128)(2,1)} %get-tuple-element.1106) | copy-start | bytes 4718596 | tf_op jit(solution)/shard_map/while
  469.5 8.7 copy-start.10
  470.7 7.6 copy-start.22
  470.7 7.6 copy-start.56
  488.5 21.5 %slice-start.7 = ((s8[4718592]{0:T(1024)(128)(4,1)}), s8[4194304]{0:T(1024)(128)(4,1)S(1)}, s32[]{:S(2)}) async-start(s8[4718592]{0:T(1024)(128)(4,1)} %bitcast.193), calls=%async_computation.19 | async-start | bytes 8388608 | tf_op jit(solution)/shard_map/while
  491.0 19.0 %slice-start.8 = ((s8[4718592]{0:T(1024)(128)(4,1)}), s8[524288]{0:T(1024)(128)(4,1)S(1)}, s32[]{:S(2)}) async-start(s8[4718592]{0:T(1024)(128)(4,1)} %bitcast.193), calls=%async_computation.20 | async-start | bytes 1048576 | tf_op jit(solution)/shard_map/while
  520.1 14.2 %copy-start.9 = (f32[768,768]{1,0:T(8,128)S(1)}, f32[768,768]{1,0:T(8,128)}, u32[]{:S(2)}) copy-start(f32[768,768]{1,0:T(8,128)} %get-tuple-element.1069) | copy-start | bytes 7077892 | tf_op jit(solution)/shard_map/while
  520.1 14.2 %copy-start.21 = (bf16[1024,768]{0,1:T(8,128)(2,1)S(1)}, bf16[1024,768]{0,1:T(8,128)(2,1)}, u32[]{:S(2)}) copy-start(bf16[1024,768]{0,1:T(8,128)(2,1)} %get-tuple-element.1106) | copy-start | bytes 4718596 | tf_op jit(solution)/shard_map/while
  535.1 8.7 copy-start.10
  536.2 7.5 copy-start.22
  536.2 7.6 copy-start.56
  546.2 243.3 %reduce-scatter.5.cloned.1.call-start = ((), (), s32[]{:S(2)}) async-start(), calls=%async_computation.8 | async-start | bytes 7299072 | tf_op jit(solution)/shard_map/reduce_scatter | solution.py:335
  599.8 8.2 copy-start.28
  599.9 8.2 copy-start.54
  660.2 8.1 copy-start.28
  660.2 8.1 copy-start.54
  670.7 259.8 %reduce-scatter.9.cloned.1.call-start = ((), (), s32[]{:S(2)}) async-start(), calls=%async_computation.10 | async-start | bytes 9732096 | tf_op jit(solution)/shard_map/reduce_scatter | solution.py:337
  671.5 400.1 %reduce-scatter.11.cloned.1.call-start = ((), (), s32[]{:S(2)}) async-start(), calls=%async_computation.11 | async-start | bytes 9732096 | tf_op jit(solution)/shard_map/reduce_scatter | solution.py:338
  1075.2 44.9 %copy-start.51 = (f32[48]{0:T(128)S(1)}, f32[48]{0:T(128)}, u32[]{:S(2)}) copy-start(f32[48]{0:T(128)} %param.45) | copy-start | bytes 580
  1075.2 44.9 %copy-start.52 = (f32[48]{0:T(128)S(1)}, f32[48]{0:T(128)}, u32[]{:S(2)}) copy-start(f32[48]{0:T(128)} %param.57) | copy-start | bytes 580
  1075.2 44.9 %copy-start.53 = (f32[48]{0:T(128)S(1)}, f32[48]{0:T(128)}, u32[]{:S(2)}) copy-start(f32[48]{0:T(128)} %param.51) | copy-start | bytes 580
  1075.3 45.5 %copy-start.47 = (f32[240]{0:T(256)S(1)}, f32[240]{0:T(256)}, u32[]{:S(2)}) copy-start(f32[240]{0:T(256)} %param.44) | copy-start | bytes 2884
  1075.3 45.5 %copy-start.48 = (f32[240]{0:T(256)S(1)}, f32[240]{0:T(256)}, u32[]{:S(2)}) copy-start(f32[240]{0:T(256)} %param.56) | copy-start | bytes 2884
  1075.3 45.5 %copy-start.49 = (f32[240]{0:T(256)S(1)}, f32[240]{0:T(256)}, u32[]{:S(2)}) copy-start(f32[240]{0:T(256)} %param.50) | copy-start | bytes 2884
  1075.3 46.1 %copy-start.29 = (f32[96,768]{1,0:T(8,128)S(1)}, f32[96,768]{1,0:T(8,128)}, u32[]{:S(2)}) copy-start(f32[96,768]{1,0:T(8,128)} %param.43) | copy-start | bytes 884740
  1075.3 46.1 %copy-start.32 = (f32[96,768]{1,0:T(8,128)S(1)}, f32[96,768]{1,0:T(8,128)}, u32[]{:S(2)}) copy-start(f32[96,768]{1,0:T(8,128)} %reduce-scatter.11.cloned.1.call-done) | copy-start | bytes 884740
  1075.3 46.1 %copy-start.37 = (f32[96,768]{1,0:T(8,128)S(1)}, f32[96,768]{1,0:T(8,128)}, u32[]{:S(2)}) copy-start(f32[96,768]{1,0:T(8,128)} %param.55) | copy-start | bytes 884740
  1075.3 48.1 %copy-start.30 = (f32[24,3072]{1,0:T(8,128)S(1)}, f32[24,3072]{1,0:T(8,128)}, u32[]{:S(2)}) copy-start(f32[24,3072]{1,0:T(8,128)} %param.42) | copy-start | bytes 884740
  1075.3 48.1 %copy-start.31 = (f32[24,3072]{1,0:T(8,128)S(1)}, f32[24,3072]{1,0:T(8,128)}, u32[]{:S(2)}) copy-start(f32[24,3072]{1,0:T(8,128)} %reduce-scatter.9.cloned.1.call-done) | copy-start | bytes 884740
  1075.3 51.9 %copy-start.1 = (bf16[1024,768]{1,0:T(8,128)(2,1)S(1)}, bf16[1024,768]{1,0:T(8,128)(2,1)}, u32[]{:S(2)}) copy-start(bf16[1024,768]{1,0:T(8,128)(2,1)} %param.34) | copy-start | bytes 4718596
  1079.7 46.6 %copy-start.33 = (f32[24,2304]{1,0:T(8,128)S(1)}, f32[24,2304]{1,0:T(8,128)}, u32[]{:S(2)}) copy-start(f32[24,2304]{1,0:T(8,128)} %reduce-scatter.5.cloned.1.call-done) | copy-start | bytes 663556
  1079.7 46.6 %copy-start.34 = (f32[24,2304]{1,0:T(8,128)S(1)}, f32[24,2304]{1,0:T(8,128)}, u32[]{:S(2)}) copy-start(f32[24,2304]{1,0:T(8,128)} %param.40) | copy-start | bytes 663556
  (59 other events, 203.8 us)
Sparse Core Ops, SparseCore 0:
  11.5 56.7 all-gather.6
  71.8 58.9 all-gather.4
  134.3 62.3 all-gather.10
  200.0 61.9 all-gather.8
  546.3 97.9 reduce-scatter.6
  670.9 118.5 reduce-scatter.4
  795.4 135.1 reduce-scatter.8
  936.4 135.1 reduce-scatter.10
where the time goes:
time: 1140 us
  waiting for transfers between devices  519 us (46%)
  matrix products  219 us (19%)
  local copies, waits for them, and re-layouts  150 us (13%)
  blocking collectives  122 us (11%)
  other arithmetic  67.6 us (6%)
  loops' own time  31.8 us (3%)
  between operations  25.9 us (2%)
    all_gather x4, waiting for transfers between devices, body(): lax.all_gather(shortened(lowered), 'dp', axis=0, tiled=True)  186 us
    reduce_scatter x1, waiting for transfers between devices, body(): lax.psum_scatter(totals[3], 'dp', scatter_dimension=0, tiled=True)  139 us
    reduce_scatter x1, waiting for transfers between devices, body(): lax.psum_scatter(totals[2], 'dp', scatter_dimension=0, tiled=True)  138 us
    unnamed x2, blocking collectives  82.3 us
    reduce_scatter x1, waiting for transfers between devices, body(): lax.psum_scatter(totals[0], 'dp', scatter_dimension=0, tiled=True)  54.1 us
    psum x1, blocking collectives, body(): total_squares = lax.psum(local_squares, 'dp')  39.6 us
    dot_general x2, matrix products, backward_tail(): jnp.einsum('rd,fd->rf', d_ffn, w_down, preferred_element_type=jnp.float32)  38 us
    dot_general x2, matrix products, forward_block(): jnp.dot(hidden_low, w_down, preferred_element_type=jnp.float32) + b_down  32 us
  transfers between devices with their start and end apart: 8, of which 6 were waited for; matrix products, arithmetic and copies ran while one was open for 15% of the time, Pallas kernels for 0%

commit v1 on v0

v1 whole, which is shorter than its diff:
```python
import functools

import jax
import jax.numpy as jnp
from jax import lax
from jax.experimental import pallas as pl
from jax.experimental.pallas import tpu as pltpu
from jax.sharding import PartitionSpec as P

HEAD_DIM = 64
CLUSTER = 128
PAIR = 2 * HEAD_DIM
ROWS = 256
BIAS_ROWS = 8

EPSILON = 1e-06
CLIP_BOUND = 1.0
BETA_ONE = 0.9
BETA_TWO = 0.999
ADAM_EPS = 1e-08
DECAY = 0.01
ROOT_HALF = 0.5**0.5
DENSITY = 0.3989422804014327

BF = jnp.bfloat16
F32 = jnp.float32
VMEM_LIMIT = 60 * 1024 * 1024


def dot(left, right):
    return lax.dot_general(left, right, (((1,), (0,)), ((), ())), preferred_element_type=F32)


def dot_nt(left, right):
    return lax.dot_general(left, right, (((1,), (1,)), ((), ())), preferred_element_type=F32)


def dot_tn(left, right):
    return lax.dot_general(left, right, (((0,), (0,)), ((), ())), preferred_element_type=F32)


def whole(shape):
    return pl.BlockSpec(shape, lambda *_: (0,) * len(shape))


def standardize(values):
    centred = values - jnp.mean(values, axis=-1, keepdims=True)
    spread = jnp.mean(centred * centred, axis=-1, keepdims=True)
    inverse = lax.rsqrt(spread + EPSILON)
    return centred * inverse, inverse


def norm_back(upstream, gain, xhat, inverse):
    scaled = upstream * gain
    mean_one = jnp.mean(scaled, axis=-1, keepdims=True)
    mean_two = jnp.mean(scaled * xhat, axis=-1, keepdims=True)
    return (scaled - mean_one - xhat * mean_two) * inverse


def column_sum(values):
    return jnp.sum(values, axis=0, keepdims=True)


def lane_masks(rows):
    lane = lax.broadcasted_iota(jnp.int32, (rows, PAIR), 1)
    return lane < HEAD_DIM


def stack_heads(block, low_half):
    zero = jnp.zeros_like(block)
    return jnp.concatenate(
        [jnp.where(low_half, block, zero), jnp.where(low_half, zero, block)], axis=0
    )


def pair_probs(query, key_stack):
    scaled = dot_nt(query, key_stack) * HEAD_DIM ** (-0.5)
    parts = []
    for half in range(2):
        part = scaled[:, half * CLUSTER : (half + 1) * CLUSTER]
        weight = jnp.exp(part - jnp.max(part, axis=-1, keepdims=True))
        parts.append(weight / jnp.sum(weight, axis=-1, keepdims=True))
    return parts


def attention_forward(qkv, context, rows, width):
    low_half = lane_masks(CLUSTER)
    for start in range(0, rows, CLUSTER):
        span = slice(start, start + CLUSTER)
        for col in range(0, width, PAIR):
            query = qkv[span, col : col + PAIR]
            keys = stack_heads(qkv[span, width + col : width + col + PAIR], low_half)
            vals = stack_heads(qkv[span, 2 * width + col : 2 * width + col + PAIR], low_half)
            probs = jnp.concatenate(pair_probs(query, keys), axis=1).astype(BF)
            context[span, col : col + PAIR] = dot(probs, vals).astype(BF)


def attention_backward(qkv, d_context, d_qkv, row, rows, width):
    low_half = lane_masks(CLUSTER)
    for start in range(0, rows, CLUSTER):
        span = slice(start, start + CLUSTER)
        out_span = pl.ds(pl.multiple_of(row + start, CLUSTER), CLUSTER)
        for col in range(0, width, PAIR):
            query = qkv[span, col : col + PAIR]
            keys = stack_heads(qkv[span, width + col : width + col + PAIR], low_half)
            vals = stack_heads(qkv[span, 2 * width + col : 2 * width + col + PAIR], low_half)
            d_ctx = d_context[span, col : col + PAIR]
            probs = pair_probs(query, keys)
            d_probs = dot_nt(d_ctx, vals)
            d_raw = []
            for half in range(2):
                part = d_probs[:, half * CLUSTER : (half + 1) * CLUSTER]
                mixed = probs[half] * part
                total = jnp.sum(mixed, axis=-1, keepdims=True)
                d_raw.append(((mixed - probs[half] * total) * HEAD_DIM ** (-0.5)).astype(BF))
            d_raw = jnp.concatenate(d_raw, axis=1)
            probs_low = jnp.concatenate(probs, axis=1).astype(BF)
            d_query = dot(d_raw, keys)
            d_key = dot_tn(d_raw, query)
            d_val = dot_tn(probs_low, d_ctx)
            d_key = jnp.where(low_half, d_key[:CLUSTER], d_key[CLUSTER:])
            d_val = jnp.where(low_half, d_val[:CLUSTER], d_val[CLUSTER:])
            d_qkv[out_span, col : col + PAIR] = d_query.astype(BF)
            d_qkv[out_span, width + col : width + col + PAIR] = d_key.astype(BF)
            d_qkv[out_span, 2 * width + col : 2 * width + col + PAIR] = d_val.astype(BF)


def attn_forward_kernel(width, x_ref, w_ref, vec_ref, gain_ref, qkv_ref, ctx_ref, xhat_ref, inv_ref):
    x_low = x_ref[...]
    for part in range(3):
        value = dot(x_low, w_ref[part])
        if part != 1:
            offset = 0 if part == 0 else width
            value = value + vec_ref[:, offset : offset + width]
        qkv_ref[:, part * width : (part + 1) * width] = value.astype(BF)
    attention_forward(qkv_ref, ctx_ref, x_ref.shape[0], width)
    attn = dot(ctx_ref[...], w_ref[3]) + vec_ref[:, 2 * width : 3 * width]
    xhat, inverse = standardize(x_low.astype(F32) + attn)
    xhat_ref[...] = xhat
    inv_ref[...] = jnp.broadcast_to(inverse, inv_ref.shape)


def attn_forward(x, w_attn, vectors, gains):
    rows, width = x.shape
    row_spec = lambda cols: pl.BlockSpec((ROWS, cols), lambda i: (i, 0))
    return pl.pallas_call(
        functools.partial(attn_forward_kernel, width),
        grid=(rows // ROWS,),
        in_specs=[row_spec(width), whole(w_attn.shape), whole(vectors.shape), whole(gains.shape)],
        out_specs=[row_spec(3 * width), row_spec(width), row_spec(width), row_spec(128)],
        out_shape=[
            jax.ShapeDtypeStruct((rows, 3 * width), BF),
            jax.ShapeDtypeStruct((rows, width), BF),
            jax.ShapeDtypeStruct((rows, width), F32),
            jax.ShapeDtypeStruct((rows, 128), F32),
        ],
        compiler_params=pltpu.CompilerParams(vmem_limit_bytes=VMEM_LIMIT),
        cost_estimate=pl.CostEstimate(
            flops=8 * rows * width * width, bytes_accessed=24 * rows * width, transcendentals=0
        ),
        name="attn_forward",
    )(x, w_attn, vectors, gains)


def ffn_forward_kernel(
    width, hidden_width, live_ref, xhat_ref, c_ref, up_w, down_w, vec_ref, gain_ref,
    hid_ref, slope_ref, out_ref, dsec_ref, sums_ref, low, acc,
):
    step = pl.program_id(0)
    rows = xhat_ref.shape[0]
    chunk = up_w.shape[1]
    shift_at = 4 * width + hidden_width

    def normed_rows(span):
        return xhat_ref[span, :] * gain_ref[:, :width] + vec_ref[:, shift_at : shift_at + width]

    @pl.when(step == 0)
    def _():
        for start in range(0, rows, ROWS):
            span = slice(start, start + ROWS)
            value = normed_rows(span)
            low[span, :] = value.astype(BF)
            acc[span, :] = value + vec_ref[:, 3 * width + hidden_width : shift_at]

    b_up = vec_ref[:, pl.ds(pl.multiple_of(3 * width + step * chunk, 128), chunk)]
    for start in range(0, rows, ROWS):
        span = slice(start, start + ROWS)
        up = dot(low[span, :], up_w[...]) + b_up
        phi = 0.5 + 0.5 * lax.erf(up * ROOT_HALF)
        slope_ref[span, :] = (phi + up * (jnp.exp(-0.5 * up * up) * DENSITY)).astype(BF)
        hidden = (up * phi).astype(BF)
        hid_ref[span, :] = hidden
        acc[span, :] += dot(hidden, down_w[...])

    @pl.when(step == pl.num_programs(0) - 1)
    def _():
        live_rows = live_ref[0] * CLUSTER
        gain = gain_ref[:, width:]
        shift = vec_ref[:, shift_at + width :]
        sums = [jnp.zeros((1, width), F32) for _ in range(3)]
        for start in range(0, rows, ROWS):
            span = slice(start, start + ROWS)
            xhat, inverse = standardize(acc[span, :])
            live = lax.broadcasted_iota(jnp.int32, (ROWS, width), 0) + start < live_rows
            out_ref[span, :] = jnp.where(live, xhat * gain + shift, 0.0).astype(BF)
            c = jnp.where(live, c_ref[span, :].astype(F32), 0.0)
            d_second = norm_back(c, gain, xhat, inverse)
            dsec_ref[span, :] = d_second
            sums[0] += column_sum(d_second.astype(BF).astype(F32))
            sums[1] += column_sum(c)
            sums[2] += column_sum(c * xhat)
        sums_ref[...] = jnp.concatenate(sums + [jnp.zeros((5, width), F32)], axis=0)


def ffn_forward(live, xhat, c, w_up, w_down, vectors, gains):
    rows, width = xhat.shape
    steps = w_up.shape[0]
    hidden_width = steps * width
    chunk_out = pl.BlockSpec((rows, width), lambda i, _: (0, i))
    weight = pl.BlockSpec((None, width, width), lambda i, _: (i, 0, 0))
    return pl.pallas_call(
        functools.partial(ffn_forward_kernel, width, hidden_width),
        grid_spec=pltpu.PrefetchScalarGridSpec(
            num_scalar_prefetch=1,
            grid=(steps,),
            in_specs=[
                whole(xhat.shape), whole(c.shape), weight, weight,
                whole(vectors.shape), whole(gains.shape),
            ],
            out_specs=[
                chunk_out, chunk_out, whole((rows, width)), whole((rows, width)), whole((8, width)),
            ],
            scratch_shapes=[pltpu.VMEM((rows, width), BF), pltpu.VMEM((rows, width), F32)],
        ),
        out_shape=[
            jax.ShapeDtypeStruct((rows, hidden_width), BF),
            jax.ShapeDtypeStruct((rows, hidden_width), BF),
            jax.ShapeDtypeStruct((rows, width), BF),
            jax.ShapeDtypeStruct((rows, width), F32),
            jax.ShapeDtypeStruct((8, width), F32),
        ],
        compiler_params=pltpu.CompilerParams(vmem_limit_bytes=VMEM_LIMIT),
        cost_estimate=pl.CostEstimate(
            flops=4 * rows * width * hidden_width, bytes_accessed=40 * rows * width, transcendentals=0
        ),
        name="ffn_forward",
    )(live, xhat, c, w_up, w_down, vectors, gains)


def ffn_backward_kernel(
    width, hidden_width, dsec_ref, hid_ref, slope_ref, up_w, down_w, xhat_ref, inv_ref, vec_ref, gain_ref,
    gup_ref, gdown_ref, bup_ref, dfirst_ref, sums_ref, d_ffn, low, acc, d_up,
):
    step = pl.program_id(0)
    rows = xhat_ref.shape[0]
    shift_at = 4 * width + hidden_width

    @pl.when(step == 0)
    def _():
        for start in range(0, rows, ROWS):
            span = slice(start, start + ROWS)
            d_ffn[span, :] = dsec_ref[span, :].astype(BF)
            acc[span, :] = dsec_ref[span, :]
            normed = xhat_ref[span, :] * gain_ref[:, :width] + vec_ref[:, shift_at : shift_at + width]
            low[span, :] = normed.astype(BF)

    total = jnp.zeros((1, width), F32)
    for start in range(0, rows, ROWS):
        span = slice(start, start + ROWS)
        value = (dot_nt(d_ffn[span, :], down_w[...]) * slope_ref[span, :].astype(F32)).astype(BF)
        d_up[span, :] = value
        total += column_sum(value.astype(F32))
        acc[span, :] += dot_nt(value, up_w[...])
    bup_ref[...] = jnp.broadcast_to(total, bup_ref.shape)
    for start in range(0, width, ROWS):
        span = slice(start, start + ROWS)
        gdown_ref[span, :] = dot_tn(hid_ref[:, span], d_ffn[...]).astype(BF)
        gup_ref[span, :] = dot_tn(low[:, span], d_up[...]).astype(BF)

    @pl.when(step == pl.num_programs(0) - 1)
    def _():
        gain = gain_ref[:, :width]
        sums = [jnp.zeros((1, width), F32) for _ in range(3)]
        for start in range(0, rows, ROWS):
            span = slice(start, start + ROWS)
            d_normed = acc[span, :]
            xhat = xhat_ref[span, :]
            d_first = norm_back(d_normed, gain, xhat, inv_ref[span, :1])
            dfirst_ref[span, :] = d_first
            sums[0] += column_sum(d_first.astype(BF).astype(F32))
            sums[1] += column_sum(d_normed)
            sums[2] += column_sum(d_normed * xhat)
        sums_ref[...] = jnp.concatenate(sums + [jnp.zeros((5, width), F32)], axis=0)


def ffn_backward(d_second, hidden, slope, w_up, w_down, xhat, inverse, vectors, gains):
    rows, width = xhat.shape
    steps = w_up.shape[0]
    hidden_width = steps * width
    chunk = pl.BlockSpec((rows, width), lambda i: (0, i))
    weight = pl.BlockSpec((None, width, width), lambda i: (i, 0, 0))
    return pl.pallas_call(
        functools.partial(ffn_backward_kernel, width, hidden_width),
        grid=(steps,),
        in_specs=[
            whole(d_second.shape), chunk, chunk, weight, weight, whole(xhat.shape), whole(inverse.shape),
            whole(vectors.shape), whole(gains.shape),
        ],
        out_specs=[
            weight, weight, pl.BlockSpec((8, width), lambda i: (0, i)),
            whole((rows, width)), whole((8, width)),
        ],
        scratch_shapes=[
            pltpu.VMEM((rows, width), BF), pltpu.VMEM((rows, width), BF),
            pltpu.VMEM((rows, width), F32), pltpu.VMEM((rows, width), BF),
        ],
        out_shape=[
            jax.ShapeDtypeStruct((steps, width, width), BF),
            jax.ShapeDtypeStruct((steps, width, width), BF),
            jax.ShapeDtypeStruct((8, hidden_width), F32),
            jax.ShapeDtypeStruct((rows, width), F32),
            jax.ShapeDtypeStruct((8, width), F32),
        ],
        compiler_params=pltpu.CompilerParams(vmem_limit_bytes=VMEM_LIMIT),
        cost_estimate=pl.CostEstimate(
            flops=8 * rows * width * hidden_width, bytes_accessed=60 * rows * width, transcendentals=0
        ),
        name="ffn_backward",
    )(d_second, hidden, slope, w_up, w_down, xhat, inverse, vectors, gains)


def attn_backward_kernel(
    width, dfirst_ref, ctx_ref, qkv_ref, x_ref, w_ref, dx_ref, grad_ref, sums_ref,
    d_attn, d_ctx, d_qkv, x_all, ctx_all, totals,
):
    step = pl.program_id(0)
    block = x_ref.shape[0]
    row = pl.multiple_of(step * block, block)
    span = pl.ds(row, block)

    @pl.when(step == 0)
    def _():
        totals[...] = jnp.zeros_like(totals)

    d_low = dfirst_ref[...].astype(BF)
    d_attn[span, :] = d_low
    x_all[span, :] = x_ref[...]
    ctx_all[span, :] = ctx_ref[...]
    d_ctx[...] = dot_nt(d_low, w_ref[3]).astype(BF)
    attention_backward(qkv_ref, d_ctx, d_qkv, row, block, width)
    value = dfirst_ref[...]
    for part in range(3):
        piece = d_qkv[span, part * width : (part + 1) * width]
        value = value + dot_nt(piece, w_ref[part])
        totals[part : part + 1, :] += column_sum(piece.astype(F32))
    dx_ref[...] = value.astype(BF)

    @pl.when(step == pl.num_programs(0) - 1)
    def _():
        for start in range(0, width, ROWS):
            piece = slice(start, start + ROWS)
            for part in range(3):
                cols = slice(part * width, (part + 1) * width)
                grad_ref[part, piece, :] = dot_tn(x_all[:, piece], d_qkv[:, cols]).astype(BF)
            grad_ref[3, piece, :] = dot_tn(ctx_all[:, piece], d_attn[...]).astype(BF)
        sums_ref[...] = totals[...]


def attn_backward(d_first, context, qkv, x, w_attn):
    rows, width = x.shape
    row_spec = lambda cols: pl.BlockSpec((ROWS, cols), lambda i: (i, 0))
    return pl.pallas_call(
        functools.partial(attn_backward_kernel, width),
        grid=(rows // ROWS,),
        in_specs=[row_spec(width), row_spec(width), row_spec(3 * width), row_spec(width), whole(w_attn.shape)],
        out_specs=[row_spec(width), whole(w_attn.shape), whole((8, width))],
        scratch_shapes=[
            pltpu.VMEM((rows, width), BF), pltpu.VMEM((ROWS, width), BF),
            pltpu.VMEM((rows, 3 * width), BF), pltpu.VMEM((rows, width), BF),
            pltpu.VMEM((rows, width), BF), pltpu.VMEM((8, width), F32),
        ],
        out_shape=[
            jax.ShapeDtypeStruct((rows, width), BF),
            jax.ShapeDtypeStruct(w_attn.shape, BF),
            jax.ShapeDtypeStruct((8, width), F32),
        ],
        compiler_params=pltpu.CompilerParams(vmem_limit_bytes=VMEM_LIMIT),
        cost_estimate=pl.CostEstimate(
            flops=16 * rows * width * width, bytes_accessed=24 * rows * width, transcendentals=0
        ),
        name="attn_backward",
    )(d_first, context, qkv, x, w_attn)


def digits_of(count):
    return {32: (2, 2, 2, 4), 256: (2, 8, 4, 4)}.get(count, (count,))


def total_over(value, count):
    stride = 1
    for radix in digits_of(count):
        parts = [value]
        for offset in range(1, radix):
            perm = [(d, partner(d, stride, radix, offset)) for d in range(count)]
            parts.append(lax.ppermute(value, "dp", perm))
        if radix & (radix - 1) == 0:
            while len(parts) > 1:
                parts = [parts[i] + parts[i + 1] for i in range(0, len(parts), 2)]
        value = parts[0]
        stride *= radix
    return value


def partner(device, stride, radix, offset):
    digit = device // stride % radix
    return device + ((digit ^ offset) - digit) * stride


def to_blocks(matrix, width):
    return [matrix[:, start : start + width] for start in range(0, matrix.shape[1], width)]


def adam_update(masters, firsts, seconds, grads, grad_norm, step_count, learn_rates, base_rates):
    factor = CLIP_BOUND / jnp.maximum(grad_norm, CLIP_BOUND)
    moment = step_count[0].astype(F32)
    first_fix = 1.0 - BETA_ONE**moment
    second_fix = 1.0 - BETA_TWO**moment
    new_firsts, new_seconds, new_masters = [], [], []
    for number in range(6):
        clipped = factor * grads[number]
        first_new = BETA_ONE * firsts[number] + (1.0 - BETA_ONE) * clipped
        second_new = BETA_TWO * seconds[number] + (1.0 - BETA_TWO) * clipped * clipped
        step_rate = learn_rates[number] * base_rates[number]
        update = (
            first_new / first_fix / (jnp.sqrt(second_new / second_fix) + ADAM_EPS)
            + DECAY * masters[number]
        )
        new_firsts.append(first_new)
        new_seconds.append(second_new)
        new_masters.append(masters[number] - step_rate * update)
    return new_firsts, new_seconds, new_masters


def body(count, tokens, cotangent, cluster_order, live_clusters, step_count, learn_rates, *state):
    masters, moments_one, moments_two = state[:6], state[6:12], state[12:]
    w_qkv, w_out, w_up, w_down, biases, norm_gains = (value.astype(BF) for value in masters)
    rows, width = tokens.shape
    local = w_qkv.shape[0]
    local_down = w_down.shape[0]
    chunks = w_up.shape[1] // width
    hidden_width = chunks * width
    small = jnp.pad(
        jnp.concatenate([biases, norm_gains]),
        (0, BIAS_ROWS * width - biases.shape[0] - norm_gains.shape[0]),
    ).reshape(BIAS_ROWS, width)
    shard = jnp.concatenate(
        to_blocks(w_qkv, width) + [w_out] + to_blocks(w_up, width) + [w_down, small], axis=0
    )
    gathered = lax.all_gather(shard, "dp", axis=0, tiled=True).reshape(count, shard.shape[0], width)
    attn_rows, up_rows = 4 * local, (4 + chunks) * local
    w_attn = gathered[:, :attn_rows].reshape(count, 4, local, width)
    w_attn = w_attn.transpose(1, 0, 2, 3).reshape(4, width, width)
    up_all = gathered[:, attn_rows:up_rows].reshape(count, chunks, local, width)
    up_all = up_all.transpose(1, 0, 2, 3).reshape(chunks, width, width)
    down_all = gathered[:, up_rows : up_rows + local_down].reshape(chunks, width, width)
    small_all = gathered[:, up_rows + local_down :].reshape(count, BIAS_ROWS * width).astype(F32)
    vectors = small_all[:, : biases.shape[0]].reshape(1, -1)
    gains = small_all[:, biases.shape[0] : biases.shape[0] + norm_gains.shape[0]].reshape(1, -1)

    position = jnp.arange(rows, dtype=jnp.int32)
    select = (cluster_order[:, None] == position[None, :]).astype(BF)
    restore = (cluster_order[None, :] == position[:, None]).astype(BF)
    x = dot(select, tokens).astype(BF)
    c = dot(select, cotangent).astype(BF)

    qkv, context, xhat, inverse = attn_forward(x, w_attn, vectors, gains)
    hidden, slope, out_rows, d_second, sums_two = ffn_forward(
        live_clusters, xhat, c, up_all, down_all, vectors, gains
    )
    g_up, g_down, g_bup, d_first, sums_one = ffn_backward(
        d_second, hidden, slope, up_all, down_all, xhat, inverse, vectors, gains
    )
    ffn_bucket = jnp.concatenate(
        [
            g_up.reshape(chunks, count, local, width).transpose(1, 0, 2, 3).reshape(count, -1, width),
            g_down.reshape(count, local_down, width),
        ],
        axis=1,
    )
    ffn_grad = lax.psum_scatter(
        ffn_bucket.reshape(-1, width), "dp", scatter_dimension=0, tiled=True
    ).astype(F32)
    dx_rows, g_attn, sums_qkv = attn_backward(d_first, context, qkv, x, w_attn)
    g_bias = jnp.concatenate(
        [sums_qkv[0], sums_qkv[2], sums_one[0], g_bup[0], sums_two[0], sums_one[1], sums_two[1]]
    ).reshape(count, -1)
    g_gain = jnp.concatenate([sums_one[2], sums_two[2]]).reshape(count, -1)
    g_small = jnp.concatenate([g_bias, g_gain], axis=1)
    g_small = jnp.pad(g_small, ((0, 0), (0, BIAS_ROWS * width - g_small.shape[1])))
    attn_bucket = jnp.concatenate(
        [
            g_attn.reshape(4, count, local, width).transpose(1, 0, 2, 3).reshape(count, -1, width),
            g_small.astype(BF).reshape(count, BIAS_ROWS, width),
        ],
        axis=1,
    )
    attn_grad = lax.psum_scatter(
        attn_bucket.reshape(-1, width), "dp", scatter_dimension=0, tiled=True
    ).astype(F32)
    output = dot(restore, out_rows).astype(BF)
    input_grad = dot(restore, dx_rows).astype(BF)
    square = jnp.sum(ffn_grad * ffn_grad) + jnp.sum(attn_grad * attn_grad)
    grad_norm = jnp.sqrt(total_over(jnp.full((8, 128), square, F32), count)[0, 0])
    small_grad = attn_grad[attn_rows:].reshape(-1)
    reduced = (
        jnp.concatenate([attn_grad[part * local : (part + 1) * local] for part in range(3)], axis=1),
        attn_grad[3 * local : attn_rows],
        jnp.concatenate([ffn_grad[k * local : (k + 1) * local] for k in range(chunks)], axis=1),
        ffn_grad[chunks * local :],
        small_grad[: biases.shape[0]],
        small_grad[biases.shape[0] : biases.shape[0] + norm_gains.shape[0]],
    )
    base_rates = (width**-0.5, (width // CLUSTER) ** -0.5, width**-0.5, hidden_width**-0.5, 0.5, 0.5)
    firsts, seconds, updated = adam_update(
        masters, moments_one, moments_two, reduced, grad_norm, step_count, learn_rates, base_rates
    )
    return (output, input_grad, grad_norm.reshape(1), *firsts, *seconds, *updated)


def solution(mesh):
    state = (P("dp", None),) * 4 + (P("dp"),) * 2
    return jax.shard_map(
        functools.partial(body, mesh.size),
        mesh=mesh,
        in_specs=(P("dp", None), P("dp", None), P("dp"), P("dp"), P(), P()) + state * 3,
        out_specs=(P("dp", None), P("dp", None), P()) + state * 3,
        check_vma=False,
    )
```

time: 1140 us -> 558 us (0.49)
  matrix products: 219 us -> 14.8 us
  waiting for transfers between devices: 519 us -> 339 us
  blocking collectives: 122 us -> 0 us
  local copies, waits for them, and re-layouts: 150 us -> 31.5 us
  Pallas kernels: 0 us -> 113 us
  other arithmetic: 67.6 us -> 25.3 us
  loops' own time: 31.8 us -> 0 us
    dot_general x38 -> x4, matrix products: 219 us -> 14.8 us  [dot(): lax.dot_general(left, right, (((1,), (0,)), ((), ())), preferred_element_...]
    pallas_call x0 -> x4, Pallas kernels: none -> 113 us  [the longest x1 43.2 us: attn_backward(): pl.pallas_call(functools.partial(attn_backward_kernel, width), grid=(rows...]
    reduce_scatter x4 -> x2, waiting for transfers between devices: 331 us -> 234 us  [the longest x1 139 us: body(): lax.psum_scatter(ffn_bucket.reshape(-1, width), 'dp', scatter_dimension=0...]
    all_gather x4 -> x1, waiting for transfers between devices: 186 us -> 99.3 us  [body(): lax.all_gather(shard, 'dp', axis=0, tiled=True)]
    unnamed x2 -> x0, blocking collectives: 82.3 us -> none
    psum x1 -> x0, blocking collectives: 39.6 us -> none  [body(): total_squares = lax.psum(local_squares, 'dp')]
    reduce_sum x30 -> x2, other arithmetic: 40.5 us -> 3.32 us  [body(): square = jnp.sum(ffn_grad * ffn_grad) + jnp.sum(attn_grad * attn_grad)]
    another operation x3 -> x0, loops' own time: 31.8 us -> none  [the longest x1 30.6 us: body(): lax.fori_loop(0, block_count, forward_step, (empty_rows, qkv_init, log_in...]
  transfers between devices with their start and end apart: 8 -> 9, of which waited for: 6 -> 6; matrix products, arithmetic and copies ran while one was open for 15% -> 4% of each run, Pallas kernels for 0% -> 0%
where the time goes in v1:
time: 558 us; the launch traced here: 554 us
  waiting for transfers between devices  339 us (61%)
  Pallas kernels  113 us (20%)
  local copies, waits for them, and re-layouts  31.5 us (6%)
  other arithmetic  25.3 us (5%)
  between operations  22.9 us (4%)
  matrix products  14.8 us (3%)
  starting transfers between devices  6.96 us (1%)
    reduce_scatter x1, waiting for transfers between devices, body(): lax.psum_scatter(ffn_bucket.reshape(-1, width), 'dp', scatter_dimension=0...  139 us
    all_gather x1, waiting for transfers between devices, body(): lax.all_gather(shard, 'dp', axis=0, tiled=True)  99.3 us
    reduce_scatter x1, waiting for transfers between devices, body(): lax.psum_scatter(attn_bucket.reshape(-1, width), 'dp', scatter_dimension=...  94.9 us
    pallas_call x1, Pallas kernels, attn_backward(): pl.pallas_call(functools.partial(attn_backward_kernel, width), grid=(rows...  43.2 us
    pallas_call x1, Pallas kernels, ffn_backward(): pl.pallas_call(functools.partial(ffn_backward_kernel, width, hidden_width...  31.1 us
    pallas_call x1, Pallas kernels, ffn_forward(): pl.pallas_call(functools.partial(ffn_forward_kernel, width, hidden_width)...  22.8 us
    pallas_call x1, Pallas kernels, attn_forward(): pl.pallas_call(functools.partial(attn_forward_kernel, width), grid=(rows...  15.6 us
    dot_general x4, matrix products, dot(): lax.dot_general(left, right, (((1,), (0,)), ((), ())), preferred_element_...  14.8 us
  transfers between devices with their start and end apart: 9, of which 6 were waited for; matrix products, arithmetic and copies ran while one was open for 4% of the time, Pallas kernels for 0%

profile of v1, /device:TPU:0, one launch (start us, length us, event | category | flops | bytes accessed | tf_op | source)
XLA Modules:
  0.0 553.7 jit_solution(13139478098123054288)
XLA Ops:
  7.3 1.1 convert_element_type.54
  8.4 1.0 convert_element_type.56
  9.3 0.9 convert_dynamic-update-slice_fusion.1
  10.3 0.7 convert_element_type.58
  11.0 0.7 convert_element_type.59
  11.7 1.0 convert_dynamic-update-slice_fusion
  12.7 0.8 copy-done.7
  14.3 3.9 fusion.10.x_ref
  18.2 3.2 fusion.11.c_ref
  21.4 99.3 %all-gather.2.cloned.1.call-done = bf16[9472,768]{1,0:T(8,128)(2,1)} async-done(((bf16[296,768]{1,0:T(8,128)(2,1)}), bf16[9472,768]{1,0:T(8,128)(2,1)}) %all-gather.2.cloned.1.call-update) | async-done | bytes 14549008 | tf_op jit(solution)/shard_map/all_gather | solution.py:459
  120.6 10.1 %fusion.33 = (bf16[32,96,768]{2,1,0:T(8,128)(2,1)}, bf16[32,96,768]{2,1,0:T(8,128)(2,1)}, bf16[32,96,768]{2,1,0:T(8,128)(2,1)S(1)}) fusion(bf16[32,296,768]{2,1,0:T(8,128)(2,1)} %bitcast.45), kind=kLoop, calls=%fused_computation.81 | loop fusion | bytes 28311552 | tf_op jit(solution)/shard_map/slice | solution.py:465
  130.8 1.0 slice_convert_fusion
  132.1 2.4 copy.47
  134.5 0.7 reshape.146.vec_ref
  135.3 0.7 reshape.147.gain_ref
  135.9 4.8 copy.48
  140.7 15.6 %attn_forward.1 = (bf16[1024,2304]{1,0:T(8,128)(2,1)}, bf16[1024,768]{1,0:T(8,128)(2,1)}, f32[1024,768]{1,0:T(8,128)}, f32[1024,128]{1,0:T(8,128)}) custom-call(bf16[1024,768]{1,0:T(8,128)(2,1)} %fusion.10.x_ref, bf16[4,768,768]{2,1,0:T(8,128)(2,1)} %bitcast.51, f32[1,7680]{1,0:T(1,128)} %reshape.146.vec_ref, f32[1,1536]{1,0:T(1,128)} %reshape.147.gain_ref), custom_call_target="tpu_custom_call" | custom-call | flops 4831838208 | bytes 18874368 | tf_op jit(solution)/shard_map/attn_forward/pallas_call | solution.py:146
  156.3 22.8 %ffn_forward.1 = (bf16[1024,3072]{1,0:T(8,128)(2,1)}, bf16[1024,3072]{1,0:T(8,128)(2,1)}, bf16[1024,768]{1,0:T(8,128)(2,1)}, f32[1024,768]{1,0:T(8,128)}, f32[8,768]{1,0:T(8,128)}) custom-call(s32[1]{0:T(128)S(6)} %copy.69.live_ref, f32[1024,768]{1,0:T(8,128)} %get-tuple-element.38.xhat_ref, bf16[1024,768]{1,0:T(8,128)(2,1)} %fusion.11.c_ref, ...), custom_call_target="tpu_custom_call" | custom-call | flops 9663676416 | bytes 31457280 | tf_op jit(solution)/shard_map/ffn_forward/pallas_call | solution.py:221
  179.1 31.1 %ffn_backward.1 = (bf16[4,768,768]{2,1,0:T(8,128)(2,1)}, bf16[4,768,768]{2,1,0:T(8,128)(2,1)}, f32[8,3072]{1,0:T(8,128)}, f32[1024,768]{1,0:T(8,128)}, f32[8,768]{1,0:T(8,128)}) custom-call(f32[1024,768]{1,0:T(8,128)} %get-tuple-element.40.dsec_ref, bf16[1024,3072]{1,0:T(8,128)(2,1)} %get-tuple-element.41.hid_ref, ...), custom_call_target="tpu_custom_call" | custom-call | flops 19327352832 | bytes 47185920 | tf_op jit(solution)/shard_map/ffn_backward/pallas_call | solution.py:302
  210.3 43.2 %attn_backward.1 = (bf16[1024,768]{1,0:T(8,128)(2,1)}, bf16[4,768,768]{2,1,0:T(8,128)(2,1)}, f32[8,768]{1,0:T(8,128)}) custom-call(f32[1024,768]{1,0:T(8,128)} %get-tuple-element.44.dfirst_ref, bf16[1024,768]{1,0:T(8,128)(2,1)} %get-tuple-element.45.ctx_ref, bf16[1024,2304]{1,0:T(8,128)(2,1)} %get-tuple-element.46.qkv_ref, bf16[1024,768]{1,0:T(8,128)(2,1)} %fusion.10.x_ref, ...), custom_call_target="tpu_custom_call" | custom-call | flops 9663676416 | bytes 18874368 | tf_op jit(solution)/shard_map/attn_backward/pallas_call | solution.py:372
  253.5 0.7 convert.41
  254.3 0.9 fusion.24
  257.5 2.9 copy.50
  260.5 2.7 pad_maximum_fusion.1
  263.2 3.1 copy.49
  266.9 4.0 pad_maximum_fusion
  276.2 94.9 %reduce-scatter.5.cloned.1.call-done = bf16[104,768]{1,0:T(8,128)(2,1)} async-done(((bf16[3328,768]{1,0:T(8,128)(2,1)}), bf16[104,768]{1,0:T(8,128)(2,1)}) %reduce-scatter.5.cloned.1.call-update) | async-done | bytes 159760 | tf_op jit(solution)/shard_map/reduce_scatter | solution.py:507
  371.1 1.6 multiply_reduce_fusion.1
  372.7 139.5 %reduce-scatter.3.cloned.1.call-done = bf16[192,768]{1,0:T(8,128)(2,1)} async-done(((bf16[6144,768]{1,0:T(8,128)(2,1)}), bf16[192,768]{1,0:T(8,128)(2,1)}) %reduce-scatter.3.cloned.1.call-update) | async-done | bytes 294928 | tf_op jit(solution)/shard_map/reduce_scatter | solution.py:490
  512.1 1.7 multiply_reduce_fusion
  515.3 4.6 fusion.9
  519.9 1.5 collective-permute-start.1
  521.4 3.1 fusion.8
  524.5 0.9 collective-permute-start.2
  525.4 0.7 fusion.35
  526.2 2.1 collective-permute-done.2
  528.3 0.7 add.122
  529.0 1.0 collective-permute-start.3
  530.0 1.7 collective-permute-start.4
  531.7 1.6 collective-permute-start.5
  533.5 1.1 collective-permute-done.4
  534.5 2.6 collective-permute-done.5
  538.4 1.3 multiply_subtract_fusion.5
  539.7 1.3 multiply_subtract_fusion.4
  541.0 1.1 multiply_subtract_fusion
  542.1 1.7 multiply_subtract_fusion.3
  543.8 0.9 multiply_subtract_fusion.2
  544.7 1.1 multiply_subtract_fusion.1
  (100 shorter events, 5.0 us)
Async XLA Ops:
  7.2 7.0 %copy-start = (bf16[1024,768]{1,0:T(8,128)(2,1)S(1)}, bf16[1024,768]{1,0:T(8,128)(2,1)}, u32[]{:S(2)}) copy-start(bf16[1024,768]{1,0:T(8,128)(2,1)} %param.24) | copy-start | bytes 4718596
  7.2 113.4 %all-gather.2.cloned.1.call-start = ((), (), s32[]{:S(2)}) async-start(), calls=%async_computation.2 | async-start | bytes 15003648 | tf_op jit(solution)/shard_map/all_gather | solution.py:459
  12.7 0.8 copy-start.7
  13.5 357.5 %reduce-scatter.5.cloned.1.call-start = ((), (), s32[]{:S(2)}) async-start(), calls=%async_computation.4 | async-start | bytes 5271552 | tf_op jit(solution)/shard_map/reduce_scatter | solution.py:507
  14.2 3.9 copy-start.19
  14.3 3.9 copy-start.20
  210.2 44.0 %copy-start.17 = (f32[8,768]{1,0:T(8,128)S(1)}, f32[8,768]{1,0:T(8,128)}, u32[]{:S(2)}) copy-start(f32[8,768]{1,0:T(8,128)} %get-tuple-element.52) | copy-start | bytes 73732
  210.2 45.0 %copy-start.16 = (f32[8,768]{1,0:T(8,128)S(1)}, f32[8,768]{1,0:T(8,128)}, u32[]{:S(2)}) copy-start(f32[8,768]{1,0:T(8,128)} %get-tuple-element.54) | copy-start | bytes 73732
  263.1 3.2 slice-start
  263.2 249.0 %reduce-scatter.3.cloned.1.call-start = ((), (), s32[]{:S(2)}) async-start(), calls=%async_computation.3 | async-start | bytes 9732096 | tf_op jit(solution)/shard_map/reduce_scatter | solution.py:490
  263.2 3.7 slice-start.1
  270.9 0.8 copy-start.18
  515.2 4.7 collective-permute-start
  515.2 6.1 %copy-start.21 = (bf16[1024,768]{1,0:T(8,128)(2,1)S(1)}, bf16[1024,768]{1,0:T(8,128)(2,1)}, u32[]{:S(2)}) copy-start(bf16[1024,768]{1,0:T(8,128)(2,1)} %get-tuple-element.39) | copy-start | bytes 4718596
  519.9 4.6 collective-permute-start.1
  521.4 4.1 copy-start.3
  521.4 12.0 %copy-start.2 = (bf16[192,768]{1,0:T(8,128)(2,1)S(1)}, bf16[192,768]{1,0:T(8,128)(2,1)}, u32[]{:S(2)}) copy-start(bf16[192,768]{1,0:T(8,128)(2,1)} %reduce-scatter.3.cloned.1.call-done) | copy-start | bytes 884740
  521.4 19.6 %copy-start.4 = (f32[96,768]{1,0:T(8,128)S(1)}, f32[96,768]{1,0:T(8,128)}, u32[]{:S(2)}) copy-start(f32[96,768]{1,0:T(8,128)} %param.33) | copy-start | bytes 884740
  521.4 19.6 %copy-start.8 = (f32[96,768]{1,0:T(8,128)S(1)}, f32[96,768]{1,0:T(8,128)}, u32[]{:S(2)}) copy-start(f32[96,768]{1,0:T(8,128)} %param.45) | copy-start | bytes 884740
  521.4 19.6 %copy-start.9 = (f32[96,768]{1,0:T(8,128)S(1)}, f32[96,768]{1,0:T(8,128)}, u32[]{:S(2)}) copy-start(f32[96,768]{1,0:T(8,128)} %param.39) | copy-start | bytes 884740
  524.5 19.2 %copy-start.6 = (f32[24,2304]{1,0:T(8,128)S(1)}, f32[24,2304]{1,0:T(8,128)}, u32[]{:S(2)}) copy-start(f32[24,2304]{1,0:T(8,128)} %param.30) | copy-start | bytes 663556
  524.5 20.2 %copy-start.5 = (f32[24,3072]{1,0:T(8,128)S(1)}, f32[24,3072]{1,0:T(8,128)}, u32[]{:S(2)}) copy-start(f32[24,3072]{1,0:T(8,128)} %param.32) | copy-start | bytes 884740
  524.5 3.8 collective-permute-start.2
  525.4 20.3 %copy-start.1 = (bf16[1024,768]{1,0:T(8,128)(2,1)S(1)}, bf16[1024,768]{1,0:T(8,128)(2,1)}, u32[]{:S(2)}) copy-start(bf16[1024,768]{1,0:T(8,128)(2,1)} %param.24) | copy-start | bytes 4718596
  526.1 17.6 %copy-start.12 = (f32[24,768]{1,0:T(8,128)S(1)}, f32[24,768]{1,0:T(8,128)}, u32[]{:S(2)}) copy-start(f32[24,768]{1,0:T(8,128)} %get-tuple-element.89) | copy-start | bytes 221188
  526.1 17.6 %copy-start.13 = (f32[24,768]{1,0:T(8,128)S(1)}, f32[24,768]{1,0:T(8,128)}, u32[]{:S(2)}) copy-start(f32[24,768]{1,0:T(8,128)} %get-tuple-element.90) | copy-start | bytes 221188
  526.1 17.6 %copy-start.14 = (f32[24,2304]{1,0:T(8,128)S(1)}, f32[24,2304]{1,0:T(8,128)}, u32[]{:S(2)}) copy-start(f32[24,2304]{1,0:T(8,128)} %param.42) | copy-start | bytes 663556
  526.1 17.6 %copy-start.15 = (f32[24,2304]{1,0:T(8,128)S(1)}, f32[24,2304]{1,0:T(8,128)}, u32[]{:S(2)}) copy-start(f32[24,2304]{1,0:T(8,128)} %param.36) | copy-start | bytes 663556
  526.1 18.6 %copy-start.10 = (f32[24,3072]{1,0:T(8,128)S(1)}, f32[24,3072]{1,0:T(8,128)}, u32[]{:S(2)}) copy-start(f32[24,3072]{1,0:T(8,128)} %param.44) | copy-start | bytes 884740
  526.2 18.6 %copy-start.11 = (f32[24,3072]{1,0:T(8,128)S(1)}, f32[24,3072]{1,0:T(8,128)}, u32[]{:S(2)}) copy-start(f32[24,3072]{1,0:T(8,128)} %param.38) | copy-start | bytes 884740
  529.0 4.5 collective-permute-start.3
  530.0 4.5 collective-permute-start.4
  531.7 5.4 collective-permute-start.5
Sparse Core Ops, SparseCore 0:
  13.6 106.9 all-gather.1
  263.3 107.7 reduce-scatter.4
  377.0 135.1 reduce-scatter.2
